TPU v7x, 256 devices: a whole 4x4x8 slice. The times are simulated.
256 devices in a mesh: row: 16 (over y_hi, z), col: 16 (over x, y_lo, core).
Axes of the slice: x: 4, y: 4 (y_hi: 2, y_lo: 2; y = y_hi * 2 + y_lo), z: 8, core: 2. Of those that a mesh axis runs over, the one named last changes fastest.
Arguments:
- pair_map: bfloat16 [64, 8192, 128], P('row', 'col'), may hold values from -6 to 6
- norm_gain: float32 [128], replicated, may hold values from 0.5 to 1.5
- in_weights: bfloat16 [3, 128, 512], replicated, may hold values from -0.5 to 0.5
- head_gain: float32 [3, 128], replicated, may hold values from 0.5 to 1.5
- out_weights: bfloat16 [3, 128, 128], replicated, may hold values from -0.5 to 0.5
- trans_gain: float32 [128], replicated, may hold values from 0.5 to 1.5
- up_weight: bfloat16 [128, 512], replicated, may hold values from -0.5 to 0.5
- down_weight: bfloat16 [512, 128], replicated, may hold values from -0.25 to 0.25
Outputs:
- result: bfloat16 [64, 8192, 128], P('row', 'col')
All inputs are finite; a program needn't handle non-finite values.
Results may differ from a plain program's by a relative error of at most 0.012.
Values may be sent and summed in bfloat16 or wider, within the bound.
A program may use at most 64 MiB of HBM per device.

v0:
```python
import jax
import jax.numpy as jnp
from jax import lax
from jax.sharding import PartitionSpec as P

D = 128
HEADS = 4
HEAD = 32


epsilon = 1e-05


def from_everyone(x, axis):
    copies = jnp.broadcast_to(x, (lax.axis_size(axis), *x.shape))
    return lax.all_to_all(copies, axis, split_axis=0, concat_axis=0, tiled=True)


def of_everyone(x, axis):
    return from_everyone(x, axis).astype(jnp.float32).sum(axis=0)


def in_blocks(x, dim, length):
    before, after = (x.shape[:dim], x.shape[dim + 1 :])
    return jnp.moveaxis(x.reshape(*before, length, -1, *after), dim, 0)


def edges_of(length, count):
    lap = length // count
    if lap >= 8:
        lap -= lap % 8
    return [lap * k for k in range(1, count)]


def laid_out(parts, dim):
    lengths = list(parts.shape[1:])
    lengths[dim] *= parts.shape[0]
    return jnp.moveaxis(parts, 0, dim).reshape(lengths)


def exchange_in_pieces(x, axis, pieces, split_dim, concat_dim):
    parts = in_blocks(x, split_dim, lax.axis_size(axis))
    split_at = max(range(1, max(2, parts.ndim - 1)), key=lambda d: parts.shape[d])
    outs = []
    for share in jnp.split(parts, edges_of(parts.shape[split_at], pieces), axis=split_at):
        if share.size:
            outs.append(lax.all_to_all(share, axis, split_axis=0, concat_axis=0, tiled=True))
    return laid_out(jnp.concatenate(outs, axis=split_at), concat_dim)


def feature(values):
    return jnp.where(values > 0, values + 1.0, jnp.exp(jnp.minimum(values, 0.0)))


def normalize(values, gain):
    meansq = jnp.mean(values * values, axis=-1, keepdims=True)
    return values * lax.rsqrt(meansq + epsilon) * gain


def open_branch(normed, weight):
    width = weight.shape[0]
    flat = jnp.dot(normed.reshape(-1, width), weight, preferred_element_type=jnp.float32)
    shape = normed.shape[:-1] + (HEADS, HEAD)
    query_feat = feature(flat[:, :width]).astype(jnp.bfloat16).reshape(shape)
    key_feat = feature(flat[:, width : 2 * width]).astype(jnp.bfloat16).reshape(shape)
    value_rows = flat[:, 2 * width : 3 * width].astype(jnp.bfloat16).reshape(shape)
    gate_vals = jax.nn.sigmoid(flat[:, 3 * width :]).reshape(normed.shape)
    return (query_feat, key_feat, value_rows, gate_vals)


def close_branch(head_out, gate_vals, gain, weight):
    mixed_out = (normalize(head_out.reshape(gate_vals.shape), gain) * gate_vals).astype(
        jnp.bfloat16
    )
    width = weight.shape[0]
    projected = jnp.dot(mixed_out.reshape(-1, width), weight, preferred_element_type=jnp.float32)
    return projected.reshape(gate_vals.shape).astype(jnp.bfloat16)


def shards(
    pair_map, norm_gain, in_weights, head_gain, out_weights, trans_gain, up_weight, down_weight
):
    row_count = pair_map.shape[0]
    widened = pair_map.astype(jnp.float32)
    normed = normalize(widened, norm_gain).astype(jnp.bfloat16)
    row_parts = []
    partials = []
    for branch in range(2):
        query_feat, key_feat, value_rows, gate_vals = open_branch(normed, in_weights[branch])
        partial_state = jnp.einsum(
            "rcha,rchb->rahb", key_feat, value_rows, preferred_element_type=jnp.float32
        )
        partials.append(partial_state.reshape(row_count * HEAD, D))
        row_parts.append((query_feat, gate_vals))
    first_sum, second_sum = (
        of_everyone(partials[0].astype(jnp.bfloat16), "col").astype(jnp.float32),
        of_everyone(partials[1].astype(jnp.bfloat16), "col").astype(jnp.float32),
    )
    first_state = first_sum.astype(jnp.bfloat16)
    second_state = second_sum.astype(jnp.bfloat16)
    row_outputs = []
    for branch, states in enumerate((first_state, second_state)):
        query_feat, gate_vals = row_parts[branch]
        states = states.reshape(row_count, HEAD, HEADS, HEAD)
        head_out = jnp.einsum(
            "rcha,rahb->rchb", query_feat, states, preferred_element_type=jnp.float32
        )
        row_outputs.append(
            close_branch(head_out, gate_vals, head_gain[branch], out_weights[branch])
        )
    regrouped = exchange_in_pieces(normed, "row", 2, 1, 0)
    query_feat, key_feat, value_rows, gate_vals = open_branch(regrouped, in_weights[2])
    states = jnp.einsum(
        "rcha,rchb->chab", key_feat, value_rows, preferred_element_type=jnp.float32
    ).astype(jnp.bfloat16)
    head_out = jnp.einsum("rcha,chab->rchb", query_feat, states, preferred_element_type=jnp.float32)
    column_out = close_branch(head_out, gate_vals, head_gain[2], out_weights[2])
    third_out = lax.all_to_all(column_out, "row", split_axis=0, concat_axis=1, tiled=True)
    updated = (
        widened
        + row_outputs[0].astype(jnp.float32)
        + row_outputs[1].astype(jnp.float32)
        + third_out.astype(jnp.float32)
    )
    trans_in = normalize(updated, trans_gain).astype(jnp.bfloat16)
    hidden = jax.nn.silu(
        jnp.dot(trans_in.reshape(-1, D), up_weight, preferred_element_type=jnp.float32)
    ).astype(jnp.bfloat16)
    lowered = jnp.dot(hidden, down_weight, preferred_element_type=jnp.float32).reshape(
        updated.shape
    )
    return (updated + lowered).astype(jnp.bfloat16)


def solution(mesh):
    in_specs = (P("row", "col", None), P(), P(), P(), P(), P(), P(), P())
    out_specs = P("row", "col", None)
    return jax.shard_map(shards, mesh=mesh, in_specs=in_specs, out_specs=out_specs, check_vma=False)
```

profile of v0, /device:TPU:32, one launch (start us, length us, event | category | flops | bytes accessed | tf_op | source)
XLA Modules:
  0.0 122.1 jit_solution(2017225571486715361)
XLA Ops:
  0.0 1.4 %fusion.24 = f32[4,512]{1,0:T(4,128)S(1)} fusion(bf16[4,512,128]{2,1,0:T(8,128)(2,1)} %param.8), kind=kLoop, calls=%fused_computation.26 | loop fusion | flops 784384 | bytes 532480 | tf_op jit(solution)/shard_map/reduce_sum | solution.py:56
  1.5 1.4 %fusion.26 = bf16[4,512,128]{2,1,0:T(8,128)(2,1)S(1)} fusion(bf16[4,512,128]{2,1,0:T(8,128)(2,1)} %param.8, f32[128]{0:T(128)} %param.9, f32[4,512]{1,0:T(4,128)S(1)} %add_rsqrt_fusion.2), kind=kLoop, calls=%fused_computation.28 | loop fusion | flops 1048576 | bytes 1057280 | tf_op jit(solution)/shard_map/convert_element_type | solution.py:85
  2.9 0.9 fusion.66
  3.8 11.2 %all-to-all-start.2 = ((bf16[16,4,16,128]{3,2,1,0:T(8,128)(2,1)}), bf16[16,4,16,128]{3,2,1,0:T(8,128)(2,1)S(1)}, u32[]{:S(2)}, u32[]{:S(2)}) async-start(bf16[16,4,16,128]{3,2,1,0:T(8,128)(2,1)} %get-tuple-element.11), calls=%async_computation.2 | async-start | bytes 524288 | tf_op jit(solution)/shard_map/all_to_all | solution.py:47
  15.0 0.7 fusion.50
  15.7 0.5 select_convert_fusion.3
  16.2 1.5 %copy-done.2 = f32[2048,512]{1,0:T(8,128)} copy-done((f32[2048,512]{1,0:T(8,128)}, f32[2048,512]{1,0:T(8,128)S(1)}, u32[]{:S(2)}) %copy-start.2) | copy-done | bytes 4194328
  17.8 2.6 %fusion.52 = f32[2048,512]{1,0:T(8,128)} fusion(bf16[2048,128]{1,0:T(8,128)(2,1)S(1)} %bitcast.94, bf16[3,128,512]{2,1,0:T(8,128)(2,1)S(1)} %copy-done.6), kind=kOutput, calls=%fused_computation.73 | convolution fusion | flops 268435456 | bytes 4849664 | tf_op jit(solution)/shard_map/dot_general | solution.py:62
  20.7 0.4 reshape.154
  21.1 0.2 copy.90
  21.3 0.4 reshape.153
  21.7 2.0 %select_convert_fusion.5 = (bf16[2048,128]{1,0:T(8,128)(2,1)S(1)}, bf16[2048,128]{1,0:T(8,128)(2,1)S(1)}) fusion(f32[2048,512]{1,0:T(8,128)} %fusion.52), kind=kLoop, calls=%fused_computation.57 | loop fusion | flops 2621440 | bytes 3145728 | tf_op jit(solution)/shard_map/convert_element_type | solution.py:65
  23.7 2.8 %all-to-all-done.2 = bf16[16,4,16,128]{3,2,1,0:T(8,128)(2,1)S(1)} async-done(((bf16[16,4,16,128]{3,2,1,0:T(8,128)(2,1)}), bf16[16,4,16,128]{3,2,1,0:T(8,128)(2,1)S(1)}, u32[]{:S(2)}, u32[]{:S(2)}) %all-to-all-start.2) | async-done | bytes 262176 | tf_op jit(solution)/shard_map/all_to_all | solution.py:47
  26.5 6.9 %all-to-all-start.3 = ((bf16[16,4,16,128]{3,2,1,0:T(8,128)(2,1)}), bf16[16,4,16,128]{3,2,1,0:T(8,128)(2,1)}, u32[]{:S(2)}, u32[]{:S(2)}) async-start(bf16[16,4,16,128]{3,2,1,0:T(8,128)(2,1)} %get-tuple-element.12), calls=%async_computation.3 | async-start | bytes 524288 | tf_op jit(solution)/shard_map/all_to_all | solution.py:47
  33.4 1.1 fusion.23
  34.4 1.3 %slice.170 = bf16[2048,128]{1,0:T(8,128)(2,1)S(1)} slice(f32[2048,512]{1,0:T(8,128)} %fusion.52), slice={[0:2048], [256:384]} | slice | bytes 1048576 | tf_op jit(solution)/shard_map/slice | solution.py:66
  35.7 1.0 copy.94
  36.7 0.7 convert_element_type.113
  37.5 0.2 copy.95
  37.7 0.4 reshape.156
  38.1 0.2 copy.81
  38.3 0.4 reshape.149
  38.7 0.2 copy.80
  38.9 0.4 reshape.148
  39.3 0.4 fusion.22
  39.8 0.7 convert_element_type.105
  40.8 1.2 reshape.151
  42.0 2.7 %all-to-all-done.3 = bf16[16,4,16,128]{3,2,1,0:T(8,128)(2,1)} async-done(((bf16[16,4,16,128]{3,2,1,0:T(8,128)(2,1)}), bf16[16,4,16,128]{3,2,1,0:T(8,128)(2,1)}, u32[]{:S(2)}, u32[]{:S(2)}) %all-to-all-start.3) | async-done | bytes 262176 | tf_op jit(solution)/shard_map/all_to_all | solution.py:47
  44.7 0.9 broadcast_in_dim.5
  45.6 4.5 %all-to-all-start.1 = ((bf16[16,128,128]{2,1,0:T(8,128)(2,1)}), bf16[16,128,128]{2,1,0:T(8,128)(2,1)S(1)}, u32[]{:S(2)}, u32[]{:S(2)}) async-start(bf16[16,128,128]{2,1,0:T(8,128)(2,1)} %broadcast_in_dim.5), calls=%async_computation.1 | async-start | bytes 1048576 | tf_op jit(solution)/shard_map/all_to_all | solution.py:16
  50.2 1.0 pad_maximum_fusion
  51.2 1.6 %fusion.48 = f32[2048,512]{1,0:T(8,128)S(1)} fusion(bf16[2048,128]{1,0:T(8,128)(2,1)S(1)} %bitcast.102, bf16[3,128,512]{2,1,0:T(8,128)(2,1)} %param.10), kind=kOutput, calls=%fused_computation.69 | convolution fusion | flops 268435456 | bytes 4849664 | tf_op jit(solution)/shard_map/dot_general | solution.py:62
  52.8 0.5 select_convert_fusion.1
  53.3 1.5 %copy-done.1 = f32[2048,512]{1,0:T(8,128)} copy-done((f32[2048,512]{1,0:T(8,128)}, f32[2048,512]{1,0:T(8,128)S(1)}, u32[]{:S(2)}) %copy-start.1) | copy-done | bytes 4194328
  54.9 1.9 %reshape.170 = bf16[64,32,4,32]{3,2,1,0:T(4,128)(2,1)} reshape(bf16[2048,128]{1,0:T(8,128)(2,1)S(1)} %get-tuple-element.9) | data formatting | bytes 1048576 | tf_op jit(solution)/shard_map/reshape | solution.py:65
  56.7 1.8 %reshape.172 = bf16[64,32,4,32]{3,2,1,0:T(4,128)(2,1)} reshape(bf16[2048,128]{1,0:T(8,128)(2,1)S(1)} %get-tuple-element.10) | data formatting | bytes 1048576 | tf_op jit(solution)/shard_map/reshape | solution.py:64
  58.5 1.8 %reshape.171 = bf16[64,32,4,32]{3,2,1,0:T(4,128)(2,1)} reshape(bf16[2048,128]{1,0:T(8,128)(2,1)S(1)} %slice.168) | data formatting | bytes 1048576 | tf_op jit(solution)/shard_map/reshape | solution.py:66
  60.3 7.2 %multiply_reduce_fusion = (f32[64,32]{0,1:T(8,128)S(1)}, f32[64,32,4,32]{0,3,2,1:T(8,128)S(1)}) fusion(bf16[64,32,4,32]{3,2,1,0:T(4,128)(2,1)} %reshape.172, bf16[64,32,4,32]{3,2,1,0:T(4,128)(2,1)} %reshape.171, bf16[64,32,4,32]{3,2,1,0:T(4,128)(2,1)} %reshape.170), kind=kOutput, calls=%fused_computation.6 | convolution fusion | flops 34207744 | bytes 2629632 | tf_op jit(solution)/shard_map/rcha,chab->rchb/dot_general | solution.py:116
  67.5 4.6 %copy.119 = f32[64,32,4,32]{3,2,1,0:T(4,128)} copy(f32[64,32,4,32]{0,3,2,1:T(8,128)S(1)} %get-tuple-element.17) | data formatting | bytes 2097152 | tf_op jit(solution)/shard_map/reshape | solution.py:72
  72.1 3.7 %reshape.173 = f32[2048,128]{1,0:T(8,128)S(1)} reshape(f32[64,32,4,32]{3,2,1,0:T(4,128)} %copy.119) | data formatting | bytes 2097152 | tf_op jit(solution)/shard_map/reshape | solution.py:72
  76.0 0.9 broadcast_in_dim.4
  76.9 5.8 %all-to-all-start = ((bf16[16,128,128]{2,1,0:T(8,128)(2,1)}), bf16[16,128,128]{2,1,0:T(8,128)(2,1)}, u32[]{:S(2)}, u32[]{:S(2)}) async-start(bf16[16,128,128]{2,1,0:T(8,128)(2,1)} %broadcast_in_dim.4), calls=%async_computation | async-start | bytes 1048576 | tf_op jit(solution)/shard_map/all_to_all | solution.py:16
  82.9 0.4 multiply_reduce_fusion.2
  83.3 0.7 copy.98
  83.9 0.3 copy.123
  84.3 0.3 copy.99
  84.7 2.6 %fusion.40 = (bf16[2048,128]{1,0:T(8,128)(2,1)}, bf16[2048,128]{1,0:T(8,128)(2,1)S(1)}) fusion(f32[2048,512]{1,0:T(8,128)} %copy-done.2, f32[2048,128]{1,0:T(8,128)S(1)} %copy.99, f32[128]{0:T(128)S(1)} %get-tuple-element.15, f32[2048]{0:T(1024)S(1)} %bitcast.107, f32[2048,512]{1,0:T(8,128)} %copy-done.1, f32[128]{0:T(128)S(1)} %get-tuple-element.14, ...), kind=kLoop, calls=%fused_computation.59 | loop fusion | flops 3670016 | bytes 5260288 | tf_op jit(solution)/shard_map/convert_element_type | solution.py:72
  87.3 1.1 convolution_convert_fusion
  88.4 5.2 %all-to-all-done = bf16[16,128,128]{2,1,0:T(8,128)(2,1)} async-done(((bf16[16,128,128]{2,1,0:T(8,128)(2,1)}), bf16[16,128,128]{2,1,0:T(8,128)(2,1)}, u32[]{:S(2)}, u32[]{:S(2)}) %all-to-all-start) | async-done | bytes 524320 | tf_op jit(solution)/shard_map/all_to_all | solution.py:16
  93.6 7.5 %all-to-all-start.4 = ((bf16[64,32,128]{2,1,0:T(8,128)(2,1)}), bf16[64,32,128]{2,1,0:T(8,128)(2,1)}, u32[]{:S(2)}, u32[]{:S(2)}) async-start(bf16[64,32,128]{2,1,0:T(8,128)(2,1)} %convolution_convert_fusion), calls=%async_computation.4 | async-start | bytes 1048576 | tf_op jit(solution)/shard_map/all_to_all | solution.py:118
  101.1 1.1 reduce_sum.70
  102.3 0.4 multiply_reduce_fusion.3
  102.7 0.7 copy.88
  103.4 0.3 copy.121
  103.7 0.3 copy.89
  104.1 0.3 copy-done.4
  104.4 0.3 fusion.17
  104.7 1.6 %fusion.39 = bf16[2048,128]{1,0:T(8,128)(2,1)S(1)} fusion(f32[2048,512]{1,0:T(8,128)} %fusion.52, f32[2048,128]{1,0:T(8,128)S(1)} %copy.89, f32[128]{0:T(128)S(1)} %get-tuple-element.13, f32[2048]{0:T(1024)S(1)} %bitcast.108), kind=kLoop, calls=%fused_computation.58 | loop fusion | flops 1835008 | bytes 2630144 | tf_op jit(solution)/shard_map/convert_element_type | solution.py:72
  106.3 10.9 %all-to-all-done.4 = bf16[64,32,128]{2,1,0:T(8,128)(2,1)} async-done(((bf16[64,32,128]{2,1,0:T(8,128)(2,1)}), bf16[64,32,128]{2,1,0:T(8,128)(2,1)}, u32[]{:S(2)}, u32[]{:S(2)}) %all-to-all-start.4) | async-done | bytes 524320 | tf_op jit(solution)/shard_map/all_to_all | solution.py:118
  117.2 1.2 copy.111
  118.4 0.5 multiply_reduce_fusion.1
  119.0 0.3 multiply_convert_fusion.1
  119.4 1.8 %fusion.13 = f32[2048,128]{1,0:T(8,128)S(1)} fusion(bf16[512,128]{1,0:T(8,128)(2,1)S(1)} %copy-done, bf16[2048,128]{1,0:T(8,128)(2,1)S(1)} %bitcast.106, bf16[128,512]{1,0:T(8,128)(2,1)S(1)} %copy-done.12), kind=kOutput, calls=%fused_computation.12 | convolution fusion | flops 542113792 | bytes 1835008 | tf_op jit(solution)/shard_map/dot_general | solution.py:129
  121.2 0.9 add_convert_fusion
  (43 shorter events, 1.6 us)
Async XLA Ops:
  0.0 119.4 %copy-start = (bf16[512,128]{1,0:T(8,128)(2,1)S(1)}, bf16[512,128]{1,0:T(8,128)(2,1)}, u32[]{:S(2)}) copy-start(bf16[512,128]{1,0:T(8,128)(2,1)} %param.15) | copy-start | bytes 393220
  0.0 15.0 %copy-start.6 = (bf16[3,128,512]{2,1,0:T(8,128)(2,1)S(1)}, bf16[3,128,512]{2,1,0:T(8,128)(2,1)}, u32[]{:S(2)}) copy-start(bf16[3,128,512]{2,1,0:T(8,128)(2,1)} %param.10) | copy-start | bytes 1179652
  3.8 22.7 %all-to-all-start.2 = ((bf16[16,4,16,128]{3,2,1,0:T(8,128)(2,1)}), bf16[16,4,16,128]{3,2,1,0:T(8,128)(2,1)S(1)}, u32[]{:S(2)}, u32[]{:S(2)}) async-start(bf16[16,4,16,128]{3,2,1,0:T(8,128)(2,1)} %get-tuple-element.11), calls=%async_computation.2 | async-start | bytes 524288 | tf_op jit(solution)/shard_map/all_to_all | solution.py:47
  15.7 2.0 %copy-start.2 = (f32[2048,512]{1,0:T(8,128)}, f32[2048,512]{1,0:T(8,128)S(1)}, u32[]{:S(2)}) copy-start(f32[2048,512]{1,0:T(8,128)S(1)} %fusion.50) | copy-start | bytes 12582916
  26.5 18.2 %all-to-all-start.3 = ((bf16[16,4,16,128]{3,2,1,0:T(8,128)(2,1)}), bf16[16,4,16,128]{3,2,1,0:T(8,128)(2,1)}, u32[]{:S(2)}, u32[]{:S(2)}) async-start(bf16[16,4,16,128]{3,2,1,0:T(8,128)(2,1)} %get-tuple-element.12), calls=%async_computation.3 | async-start | bytes 524288 | tf_op jit(solution)/shard_map/all_to_all | solution.py:47
  39.3 2.7 %copy-start.10 = (f32[3,128]{1,0:T(4,128)S(1)}, f32[3,128]{1,0:T(4,128)}, u32[]{:S(2)}) copy-start(f32[3,128]{1,0:T(4,128)} %param.11) | copy-start | bytes 4612
  39.3 5.4 %copy-start.8 = (bf16[128,128]{1,0:T(8,128)(2,1)S(1)}, bf16[128,128]{1,0:T(8,128)(2,1)}, u32[]{:S(2)}) copy-start(bf16[128,128]{1,0:T(8,128)(2,1)} %convert_element_type.113) | copy-start | bytes 98308
  45.6 30.4 %all-to-all-start.1 = ((bf16[16,128,128]{2,1,0:T(8,128)(2,1)}), bf16[16,128,128]{2,1,0:T(8,128)(2,1)S(1)}, u32[]{:S(2)}, u32[]{:S(2)}) async-start(bf16[16,128,128]{2,1,0:T(8,128)(2,1)} %broadcast_in_dim.5), calls=%async_computation.1 | async-start | bytes 1048576 | tf_op jit(solution)/shard_map/all_to_all | solution.py:16
  52.8 2.0 %copy-start.1 = (f32[2048,512]{1,0:T(8,128)}, f32[2048,512]{1,0:T(8,128)S(1)}, u32[]{:S(2)}) copy-start(f32[2048,512]{1,0:T(8,128)S(1)} %fusion.48) | copy-start | bytes 12582916
  72.1 3.9 %copy-start.7 = (bf16[128,128]{1,0:T(8,128)(2,1)S(1)}, bf16[128,128]{1,0:T(8,128)(2,1)}, u32[]{:S(2)}) copy-start(bf16[128,128]{1,0:T(8,128)(2,1)} %convert_element_type.105) | copy-start | bytes 98308
  76.9 16.6 %all-to-all-start = ((bf16[16,128,128]{2,1,0:T(8,128)(2,1)}), bf16[16,128,128]{2,1,0:T(8,128)(2,1)}, u32[]{:S(2)}, u32[]{:S(2)}) async-start(bf16[16,128,128]{2,1,0:T(8,128)(2,1)} %broadcast_in_dim.4), calls=%async_computation | async-start | bytes 1048576 | tf_op jit(solution)/shard_map/all_to_all | solution.py:16
  84.7 2.7 %copy-start.9 = (bf16[3,128,128]{2,1,0:T(8,128)(2,1)S(1)}, bf16[3,128,128]{2,1,0:T(8,128)(2,1)}, u32[]{:S(2)}) copy-start(bf16[3,128,128]{2,1,0:T(8,128)(2,1)} %param.12) | copy-start | bytes 294916
  87.3 15.0 %copy-start.5 = (bf16[4,512,4,32]{1,0,3,2:T(4,128)(2,1)S(1)}, bf16[4,512,4,32]{1,0,3,2:T(4,128)(2,1)}, u32[]{:S(2)}) copy-start(bf16[4,512,4,32]{1,0,3,2:T(4,128)(2,1)} %reshape.151) | copy-start | bytes 1572868
  93.6 23.6 %all-to-all-start.4 = ((bf16[64,32,128]{2,1,0:T(8,128)(2,1)}), bf16[64,32,128]{2,1,0:T(8,128)(2,1)}, u32[]{:S(2)}, u32[]{:S(2)}) async-start(bf16[64,32,128]{2,1,0:T(8,128)(2,1)} %convolution_convert_fusion), calls=%async_computation.4 | async-start | bytes 1048576 | tf_op jit(solution)/shard_map/all_to_all | solution.py:118
  103.4 1.0 copy-start.4
  104.7 13.7 %copy-start.3 = (bf16[4,512,128]{2,1,0:T(8,128)(2,1)S(1)}, bf16[4,512,128]{2,1,0:T(8,128)(2,1)}, u32[]{:S(2)}) copy-start(bf16[4,512,128]{2,1,0:T(8,128)(2,1)} %param.8) | copy-start | bytes 1572868
  118.4 0.7 copy-start.11
  118.4 1.0 copy-start.12
where the time goes:
time: 123 us; the launch traced here: 122 us
  starting transfers between devices  35.9 us (29%)
  local copies, waits for them, and re-layouts  32.7 us (27%)
  waiting for transfers between devices  21.5 us (17%)
  matrix products  17.9 us (15%)
  other arithmetic  13.6 us (11%)
    all_to_all x2, starting transfers between devices, exchange_in_pieces(): lax.all_to_all(share, axis, split_axis=0, concat_axis=0, tiled=True)  18.1 us
    all_to_all x1, waiting for transfers between devices, shards(): lax.all_to_all(column_out, 'row', split_axis=0, concat_axis=1, tiled=True)  10.9 us
    all_to_all x2, starting transfers between devices, from_everyone(): return lax.all_to_all(copies, axis, split_axis=0, concat_axis=0, tiled=True)  10.3 us
    reshape x4, local copies, waits for them, and re-layouts, close_branch(): head_out.reshape(gate_vals.shape)  8.97 us
    all_to_all x1, starting transfers between devices, shards(): lax.all_to_all(column_out, 'row', split_axis=0, concat_axis=1, tiled=True)  7.5 us
    dot_general x1, matrix products, shards(): jnp.einsum('rcha,chab->rchb', query_feat, states, preferred_element_type=...  7.18 us
    all_to_all x2, waiting for transfers between devices, exchange_in_pieces(): lax.all_to_all(share, axis, split_axis=0, concat_axis=0, tiled=True)  5.5 us
    all_to_all x2, waiting for transfers between devices, from_everyone(): return lax.all_to_all(copies, axis, split_axis=0, concat_axis=0, tiled=True)  5.16 us
  transfers between devices with their start and end apart: 5, of which 4 were waited for; matrix products, arithmetic and copies ran while one was open for 41% of the time, Pallas kernels for 0%

commit v1 on v0

v1 whole, which is shorter than its diff:
```python
import jax
import jax.numpy as jnp
from jax import lax
from jax.experimental import pallas as pl
from jax.experimental.pallas import tpu as pltpu
from jax.sharding import PartitionSpec as P

D = 128
HEADS = 4
HEAD = 32
FF = 512
N_ROW = 16
N_COL = 16
ROW_DEV = 4
CHUNKS = 2
CHUNK = 16
EPS = 1e-05
MESH = pl.DeviceIdType.MESH
F32 = jnp.float32
BF16 = jnp.bfloat16

ROW_STEPS = [
    (1, 4), (0, 4), (1, 3), (1, 5), (0, 3), (0, 5), (1, 2), (1, 6),
    (0, 2), (0, 6), (1, 1), (1, 7), (0, 1), (0, 7), (1, 0),
]
COL_STEPS = [
    (dx, dl, dc) for dx in (2, 1, 3, 0) for dl in (1, 0) for dc in (1, 0) if (dx, dl, dc) != (0, 0, 0)
]


def dot(a, b):
    return jnp.dot(a, b, preferred_element_type=F32)


def dot_t(a, b):
    return lax.dot_general(a, b, (((1,), (1,)), ((), ())), preferred_element_type=F32)


def feature(v):
    return jnp.maximum(v, 0.0) + jnp.exp(jnp.minimum(v, 0.0))


def sigmoid(v):
    return 0.5 * jnp.tanh(0.5 * v) + 0.5


def normalize(v, gain):
    meansq = jnp.mean(v * v, axis=-1, keepdims=True)
    return v * lax.rsqrt(meansq + EPS) * gain


def same_head(rows, columns):
    r = lax.broadcasted_iota(jnp.int32, (rows, columns), 0) % D // HEAD
    c = lax.broadcasted_iota(jnp.int32, (rows, columns), 1) % D // HEAD
    return r == c


def kernel(
    x_hbm, ng_hbm, win_hbm, hg_hbm, wout_hbm, tg_hbm, up_hbm, down_hbm,
    out_ref,
    x, ng, win, hg, wout, tg, up, down,
    wkt, q_keep, gate_keep, upd,
    part, part_in, state, col_in, col_norm, col_res, col_out, ret,
    local_sem, f_send, f_recv, r_send, r_recv, own_sem, s_send, s_recv, g_send, g_recv,
):
    row = lax.axis_index("row")
    col = lax.axis_index("col")
    y_hi, z = row // 8, row % 8
    cx, cl, cc = col // 4, (col // 2) % 2, col % 2

    def row_peer(step):
        return ((y_hi + step[0]) % 2) * 8 + (z + step[1]) % 8

    def col_peer(step):
        return ((cx + step[0]) % 4) * 4 + ((cl + step[1]) % 2) * 2 + (cc + step[2]) % 2

    loads = [
        pltpu.make_async_copy(src, dst, local_sem.at[k])
        for k, (src, dst) in enumerate(
            [
                (x_hbm, x), (ng_hbm, ng), (win_hbm, win), (hg_hbm, hg),
                (wout_hbm, wout), (tg_hbm, tg), (up_hbm, up), (down_hbm, down),
            ]
        )
    ]
    for load in loads:
        load.start()
    own_in = [
        pltpu.make_async_copy(x_hbm.at[:, row, h], col_in.at[h, row], own_sem.at[h])
        for h in range(CHUNKS)
    ]
    for copy in own_in:
        copy.start()

    barrier = pltpu.get_barrier_semaphore()
    for step in ROW_STEPS:
        pl.semaphore_signal(barrier, 1, device_id=(row_peer(step), col), device_id_type=MESH)
    for step in COL_STEPS:
        pl.semaphore_signal(barrier, 1, device_id=(row, col_peer(step)), device_id_type=MESH)
    pl.semaphore_wait(barrier, len(ROW_STEPS) + len(COL_STEPS))

    sends = []
    for h in range(CHUNKS):
        for k, step in enumerate(ROW_STEPS):
            peer = row_peer(step)
            copy = pltpu.make_async_remote_copy(
                src_ref=x_hbm.at[:, peer, h],
                dst_ref=col_in.at[h, row],
                send_sem=f_send.at[h, k],
                recv_sem=f_recv.at[h, k],
                device_id=(peer, col),
                device_id_type=MESH,
            )
            copy.start()
            sends.append(copy)
    forward = [sends[: len(ROW_STEPS)], sends[len(ROW_STEPS) :]]

    for load in loads:
        load.wait()
    for p in range(3):
        wkt[p] = win[p, :, D : 2 * D].astype(F32).T.astype(BF16)

    head_mask = same_head(D, D)

    def row_open(i, carry):
        normed = normalize(x[i].reshape(512, D).astype(F32), ng[...]).astype(BF16)
        for p in range(2):
            q_keep[p, i] = feature(dot(normed, win[p, :, :D])).astype(BF16)
            key_t = feature(dot_t(wkt[p], normed)).astype(BF16)
            tail = dot(normed, win[p, :, 2 * D :])
            gate_keep[p, i] = sigmoid(tail[:, D:])
            full = dot(key_t, tail[:, :D].astype(BF16))
            full = jnp.where(head_mask, full, 0.0).reshape(HEADS, HEAD, D).sum(axis=0)
            part[p, i] = full.astype(BF16)
        return carry

    lax.fori_loop(0, ROW_DEV, row_open, 0)

    def slice_of(ref, at):
        return ref.at[at // 8, (at // 2) % 4, pl.ds((at % 2) * 16, 16)]

    scatter = []
    for k, step in enumerate(COL_STEPS):
        peer = col_peer(step)
        copy = pltpu.make_async_remote_copy(
            src_ref=slice_of(part, peer),
            dst_ref=part_in.at[col],
            send_sem=s_send.at[k],
            recv_sem=s_recv.at[k],
            device_id=(row, peer),
            device_id_type=MESH,
        )
        copy.start()
        scatter.append(copy)
    part_in[col] = slice_of(part, col)[...]
    for copy in scatter:
        copy.wait_recv()
    total = part_in[...].astype(F32).sum(axis=0)
    slice_of(state, col)[...] = total.astype(BF16)
    gather = []
    for k, step in enumerate(COL_STEPS):
        peer = col_peer(step)
        copy = pltpu.make_async_remote_copy(
            src_ref=slice_of(state, col),
            dst_ref=slice_of(state, col),
            send_sem=g_send.at[k],
            recv_sem=g_recv.at[k],
            device_id=(row, peer),
            device_id_type=MESH,
        )
        copy.start()
        gather.append(copy)

    first_half = lax.broadcasted_iota(jnp.int32, (D, D), 0) < 64
    pair_mask = same_head(D, 2 * D)

    def column_pass(h):
        own_in[h].wait()
        for copy in forward[h]:
            copy.wait_recv()
        for t in range(4):
            block = col_in[h, 4 * t : 4 * t + 4].reshape(256, D).astype(F32)
            col_norm[256 * t : 256 * t + 256, :] = normalize(block, ng[...])
        for group in range(4):
            normed = jnp.concatenate(
                [col_norm[pl.ds(4 * group + c, 64, stride=CHUNK), :] for c in range(4)], axis=0
            ).astype(BF16)
            query = feature(dot(normed, win[2, :, :D])).astype(BF16)
            key_t = feature(dot_t(wkt[2], normed)).astype(BF16)
            tail = dot(normed, win[2, :, 2 * D :])
            value = tail[:, :D].astype(BF16)
            heads = []
            for pair in range(2):
                at = slice(D * pair, D * pair + D)
                v = value[at]
                zero = jnp.zeros_like(v)
                v2 = jnp.concatenate(
                    [jnp.where(first_half, v, zero), jnp.where(first_half, zero, v)], axis=1
                )
                s = jnp.where(pair_mask, dot(key_t[:, at], v2), 0.0).astype(BF16)
                o = dot(query[at], s)
                heads += [o[:64, :D], o[64:, D:]]
            mixed = normalize(jnp.concatenate(heads, axis=0), hg[2:3]) * sigmoid(tail[:, D:])
            res = dot(mixed.astype(BF16), wout[2])
            for c in range(4):
                col_res[pl.ds(4 * group + c, 64, stride=CHUNK), :] = res[64 * c : 64 * c + 64]
        for t in range(4):
            col_out[h, 4 * t : 4 * t + 4] = (
                col_res[256 * t : 256 * t + 256, :].astype(BF16).reshape(4, ROW_DEV, CHUNK, D)
            )
        copies = []
        for k, step in enumerate(ROW_STEPS):
            peer = row_peer(step)
            copy = pltpu.make_async_remote_copy(
                src_ref=col_out.at[h, peer],
                dst_ref=ret.at[h, row],
                send_sem=r_send.at[h, k],
                recv_sem=r_recv.at[h, k],
                device_id=(peer, col),
                device_id_type=MESH,
            )
            copy.start()
            copies.append(copy)
        ret[h, row] = col_out[h, row]
        return copies

    back = [column_pass(0)]

    for copy in gather:
        copy.wait_recv()

    def row_close(i, carry):
        acc = x[i].reshape(512, D).astype(F32)
        for p in range(2):
            s = state[p, i]
            s = jnp.concatenate([s, s, s, s], axis=0)
            s = jnp.where(head_mask, s, jnp.zeros_like(s))
            mixed = normalize(dot(q_keep[p, i], s), hg[p : p + 1]) * gate_keep[p, i]
            acc = acc + dot(mixed.astype(BF16), wout[p]).astype(BF16).astype(F32)
        upd[i] = acc.reshape(N_ROW, CHUNKS, CHUNK, D)
        return carry

    lax.fori_loop(0, ROW_DEV, row_close, 0)

    back.append(column_pass(1))

    for h in range(CHUNKS):
        for copy in back[h]:
            copy.wait_recv()

        def transition(i, carry):
            u = (upd[i, :, h] + ret[h, :, i].astype(F32)).reshape(256, D)
            t = normalize(u, tg[...]).astype(BF16)
            hid = dot(t, up[...])
            hid = (hid * sigmoid(hid)).astype(BF16)
            out_ref[i, :, h] = (u + dot(hid, down[...])).astype(BF16).reshape(N_ROW, CHUNK, D)
            return carry

        lax.fori_loop(0, ROW_DEV, transition, 0)

    for copy in sends + scatter + gather + back[0] + back[1]:
        copy.wait_send()


def shards(x, norm_gain, in_weights, head_gain, out_weights, trans_gain, up_weight, down_weight):
    any_spec = pl.BlockSpec(memory_space=pl.ANY)
    n, m = len(ROW_STEPS), len(COL_STEPS)
    dma = pltpu.SemaphoreType.DMA
    out = pl.pallas_call(
        kernel,
        out_shape=jax.ShapeDtypeStruct((ROW_DEV, N_ROW, CHUNKS, CHUNK, D), BF16),
        in_specs=[any_spec] * 8,
        out_specs=pl.BlockSpec(memory_space=pltpu.VMEM),
        scratch_shapes=[
            pltpu.VMEM((ROW_DEV, N_ROW, CHUNKS, CHUNK, D), BF16),
            pltpu.VMEM((1, D), F32),
            pltpu.VMEM((3, D, 4 * D), BF16),
            pltpu.VMEM((3, D), F32),
            pltpu.VMEM((3, D, D), BF16),
            pltpu.VMEM((1, D), F32),
            pltpu.VMEM((D, FF), BF16),
            pltpu.VMEM((FF, D), BF16),
            pltpu.VMEM((3, D, D), BF16),
            pltpu.VMEM((2, ROW_DEV, 512, D), BF16),
            pltpu.VMEM((2, ROW_DEV, 512, D), F32),
            pltpu.VMEM((ROW_DEV, N_ROW, CHUNKS, CHUNK, D), F32),
            pltpu.VMEM((2, ROW_DEV, HEAD, D), BF16),
            pltpu.VMEM((N_COL, 16, D), BF16),
            pltpu.VMEM((2, ROW_DEV, HEAD, D), BF16),
            pltpu.VMEM((CHUNKS, N_ROW, ROW_DEV, CHUNK, D), BF16),
            pltpu.VMEM((64 * CHUNK, D), F32),
            pltpu.VMEM((64 * CHUNK, D), F32),
            pltpu.VMEM((CHUNKS, N_ROW, ROW_DEV, CHUNK, D), BF16),
            pltpu.VMEM((CHUNKS, N_ROW, ROW_DEV, CHUNK, D), BF16),
            dma((8,)), dma((CHUNKS, n)), dma((CHUNKS, n)), dma((CHUNKS, n)), dma((CHUNKS, n)),
            dma((CHUNKS,)), dma((m,)), dma((m,)), dma((m,)), dma((m,)),
        ],
        compiler_params=pltpu.CompilerParams(
            collective_id=0, has_side_effects=True, vmem_limit_bytes=60 * 1024 * 1024
        ),
    )(
        x.reshape(ROW_DEV, N_ROW, CHUNKS, CHUNK, D), norm_gain.reshape(1, D), in_weights, head_gain,
        out_weights, trans_gain.reshape(1, D), up_weight, down_weight,
    )
    return out.reshape(x.shape)


def solution(mesh):
    in_specs = (P("row", "col", None), P(), P(), P(), P(), P(), P(), P())
    return jax.shard_map(
        shards, mesh=mesh, in_specs=in_specs, out_specs=P("row", "col", None), check_vma=False
    )
```

time: 123 us -> 41.6 us (0.34)
  Pallas kernels: 0 us -> 39.2 us
  starting transfers between devices: 35.9 us -> 0 us
  local copies, waits for them, and re-layouts: 32.7 us -> 1.87 us
  waiting for transfers between devices: 21.5 us -> 0 us
  matrix products: 17.9 us -> 0 us
  other arithmetic: 13.6 us -> 0 us
    pallas_call x0 -> x1, Pallas kernels: none -> 39.2 us  [shards(): pl.pallas_call(kernel, out_shape=jax.ShapeDtypeStruct((ROW_DEV, N_ROW, CH...]
    all_to_all x5 -> x0, starting transfers between devices: 35.9 us -> none  [the longest x2 18.1 us: exchange_in_pieces(): lax.all_to_all(share, axis, split_axis=0, concat_axis=0, tiled=True)]
    all_to_all x5 -> x0, waiting for transfers between devices: 21.5 us -> none  [the longest x1 10.9 us: shards(): lax.all_to_all(column_out, 'row', split_axis=0, concat_axis=1, tiled=True)]
    dot_general x12 -> x0, matrix products: 17.9 us -> none  [the longest x1 7.18 us: shards(): jnp.einsum('rcha,chab->rchb', query_feat, states, preferred_element_type=...]
    reshape x16 -> x0, local copies, waits for them, and re-layouts: 17.8 us -> none  [the longest x4 8.97 us: close_branch(): head_out.reshape(gate_vals.shape)]
    convert_element_type x8 -> x0, other arithmetic: 9.88 us -> none  [the longest x2 4.26 us: close_branch(): (normalize(head_out.reshape(gate_vals.shape), gain) * gate_vals).astype(j...]
    convert_element_type x9 -> x0, local copies, waits for them, and re-layouts: 4.68 us -> none  [the longest x2 1.78 us: shards(): partials[1].astype(jnp.bfloat16)]
    reduce_sum x3 -> x0, other arithmetic: 2.65 us -> none  [the longest x1 1.45 us: normalize(): meansq = jnp.mean(values * values, axis=-1, keepdims=True)]
  transfers between devices with their start and end apart: 5 -> 0, of which waited for: 4 -> 0; matrix products, arithmetic and copies ran while one was open for 41% -> 0% of each run, Pallas kernels for 0% -> 0%
where the time goes in v1:
time: 41.6 us; the launch traced here: 41.1 us
  Pallas kernels  39.2 us (94%)
  local copies, waits for them, and re-layouts  1.87 us (4%)
    pallas_call x1, Pallas kernels, shards(): pl.pallas_call(kernel, out_shape=jax.ShapeDtypeStruct((ROW_DEV, N_ROW, CH...  39.2 us
    unnamed x1, local copies, waits for them, and re-layouts  1.87 us

profile of v1, /device:TPU:32, one launch (start us, length us, event | category | flops | bytes accessed | tf_op | source)
XLA Modules:
  0.0 41.1 jit_solution(1882198920445257412)
XLA Ops:
  0.0 39.2 %shard_map.82 = bf16[4,16,2,16,128]{4,3,2,1,0:T(8,128)(2,1)} custom-call(bf16[4,16,2,16,128]{4,3,2,1,0:T(8,128)(2,1)} %bitcast.5, f32[1,128]{1,0:T(1,128)} %bitcast.6, bf16[3,128,512]{2,1,0:T(8,128)(2,1)} %win_hbm.1, f32[3,128]{1,0:T(4,128)} %hg_hbm.1, bf16[3,128,128]{2,1,0:T(8,128)(2,1)} %wout_hbm.1, f32[1,128]{1,0:T(1,128)} %bitcast.7, ...), custom_call_target="tpu_custom_call" | custom-call | tf_op jit(solution)/shard_map/pallas_call | solution.py:269
  39.2 1.9 %copy.10 = bf16[4,512,128]{2,1,0:T(8,128)(2,1)} copy(bf16[4,512,128]{2,1,0:T(8,128)(2,1)} %bitcast.4) | data formatting | bytes 1048576

commit v2 on v1

--- a/solution.py
+++ b/solution.py
@@ -28,6 +28,10 @@
 ]
 
 
+def arrived(ref, sem):
+    pltpu.make_async_copy(ref, ref, sem).wait()
+
+
 def dot(a, b):
     return jnp.dot(a, b, preferred_element_type=F32)
 
@@ -61,7 +65,7 @@
     x, ng, win, hg, wout, tg, up, down,
     wkt, q_keep, gate_keep, upd,
     part, part_in, state, col_in, col_norm, col_res, col_out, ret,
-    local_sem, f_send, f_recv, r_send, r_recv, own_sem, s_send, s_recv, g_send, g_recv,
+    local_sem, f_send, f_recv, r_send, r_recv, s_send, s_recv, g_send, g_recv,
 ):
     row = lax.axis_index("row")
     col = lax.axis_index("col")
@@ -75,7 +79,7 @@
         return ((cx + step[0]) % 4) * 4 + ((cl + step[1]) % 2) * 2 + (cc + step[2]) % 2
 
     loads = [
-        pltpu.make_async_copy(src, dst, local_sem.at[k])
+        pltpu.make_async_copy(src, dst, local_sem.at[int(k > 0)])
         for k, (src, dst) in enumerate(
             [
                 (x_hbm, x), (ng_hbm, ng), (win_hbm, win), (hg_hbm, hg),
@@ -85,37 +89,31 @@
     ]
     for load in loads:
         load.start()
-    own_in = [
-        pltpu.make_async_copy(x_hbm.at[:, row, h], col_in.at[h, row], own_sem.at[h])
-        for h in range(CHUNKS)
-    ]
-    for copy in own_in:
-        copy.start()
+    for h in range(CHUNKS):
+        pltpu.make_async_copy(x_hbm.at[:, row, h], col_in.at[h, row], f_recv.at[h]).start()
 
     barrier = pltpu.get_barrier_semaphore()
     for step in ROW_STEPS:
         pl.semaphore_signal(barrier, 1, device_id=(row_peer(step), col), device_id_type=MESH)
     for step in COL_STEPS:
         pl.semaphore_signal(barrier, 1, device_id=(row, col_peer(step)), device_id_type=MESH)
-    pl.semaphore_wait(barrier, len(ROW_STEPS) + len(COL_STEPS))
-
-    sends = []
+    with jax.named_scope('bar'):
+        pl.semaphore_wait(barrier, len(ROW_STEPS) + len(COL_STEPS))
+
     for h in range(CHUNKS):
-        for k, step in enumerate(ROW_STEPS):
+        for step in ROW_STEPS:
             peer = row_peer(step)
-            copy = pltpu.make_async_remote_copy(
+            pltpu.make_async_remote_copy(
                 src_ref=x_hbm.at[:, peer, h],
                 dst_ref=col_in.at[h, row],
-                send_sem=f_send.at[h, k],
-                recv_sem=f_recv.at[h, k],
+                send_sem=f_send,
+                recv_sem=f_recv.at[h],
                 device_id=(peer, col),
                 device_id_type=MESH,
-            )
-            copy.start()
-            sends.append(copy)
-    forward = [sends[: len(ROW_STEPS)], sends[len(ROW_STEPS) :]]
-
-    for load in loads:
+            ).start()
+
+    with jax.named_scope("loads"):
+      for load in loads:
         load.wait()
     for p in range(3):
         wkt[p] = win[p, :, D : 2 * D].astype(F32).T.astype(BF16)
@@ -134,50 +132,44 @@
             part[p, i] = full.astype(BF16)
         return carry
 
-    lax.fori_loop(0, ROW_DEV, row_open, 0)
+    with jax.named_scope('row_open'):
+        lax.fori_loop(0, ROW_DEV, row_open, 0, unroll=True)
 
     def slice_of(ref, at):
         return ref.at[at // 8, (at // 2) % 4, pl.ds((at % 2) * 16, 16)]
 
-    scatter = []
-    for k, step in enumerate(COL_STEPS):
+    for step in COL_STEPS:
         peer = col_peer(step)
-        copy = pltpu.make_async_remote_copy(
+        pltpu.make_async_remote_copy(
             src_ref=slice_of(part, peer),
             dst_ref=part_in.at[col],
-            send_sem=s_send.at[k],
-            recv_sem=s_recv.at[k],
+            send_sem=s_send,
+            recv_sem=s_recv,
             device_id=(row, peer),
             device_id_type=MESH,
-        )
-        copy.start()
-        scatter.append(copy)
+        ).start()
     part_in[col] = slice_of(part, col)[...]
-    for copy in scatter:
-        copy.wait_recv()
+    with jax.named_scope("rs_wait"):
+        arrived(part_in.at[: N_COL - 1], s_recv)
     total = part_in[...].astype(F32).sum(axis=0)
     slice_of(state, col)[...] = total.astype(BF16)
-    gather = []
-    for k, step in enumerate(COL_STEPS):
+    for step in COL_STEPS:
         peer = col_peer(step)
-        copy = pltpu.make_async_remote_copy(
+        pltpu.make_async_remote_copy(
             src_ref=slice_of(state, col),
             dst_ref=slice_of(state, col),
-            send_sem=g_send.at[k],
-            recv_sem=g_recv.at[k],
+            send_sem=g_send,
+            recv_sem=g_recv,
             device_id=(row, peer),
             device_id_type=MESH,
-        )
-        copy.start()
-        gather.append(copy)
+        ).start()
 
     first_half = lax.broadcasted_iota(jnp.int32, (D, D), 0) < 64
     pair_mask = same_head(D, 2 * D)
 
     def column_pass(h):
-        own_in[h].wait()
-        for copy in forward[h]:
-            copy.wait_recv()
+        with jax.named_scope("f_wait"):
+            arrived(col_in.at[h], f_recv.at[h])
         for t in range(4):
             block = col_in[h, 4 * t : 4 * t + 4].reshape(256, D).astype(F32)
             col_norm[256 * t : 256 * t + 256, :] = normalize(block, ng[...])
@@ -208,26 +200,25 @@
             col_out[h, 4 * t : 4 * t + 4] = (
                 col_res[256 * t : 256 * t + 256, :].astype(BF16).reshape(4, ROW_DEV, CHUNK, D)
             )
-        copies = []
-        for k, step in enumerate(ROW_STEPS):
-            peer = row_peer(step)
-            copy = pltpu.make_async_remote_copy(
-                src_ref=col_out.at[h, peer],
-                dst_ref=ret.at[h, row],
-                send_sem=r_send.at[h, k],
-                recv_sem=r_recv.at[h, k],
-                device_id=(peer, col),
-                device_id_type=MESH,
-            )
-            copy.start()
-            copies.append(copy)
+        for half in range(2):
+            rows = pl.ds(2 * half, 2)
+            for step in ROW_STEPS:
+                peer = row_peer(step)
+                pltpu.make_async_remote_copy(
+                    src_ref=col_out.at[h, peer, rows],
+                    dst_ref=ret.at[h, row, rows],
+                    send_sem=r_send,
+                    recv_sem=r_recv.at[h, half],
+                    device_id=(peer, col),
+                    device_id_type=MESH,
+                ).start()
         ret[h, row] = col_out[h, row]
-        return copies
-
-    back = [column_pass(0)]
-
-    for copy in gather:
-        copy.wait_recv()
+
+    with jax.named_scope("col_a"):
+        column_pass(0)
+
+    with jax.named_scope("ag_wait"):
+        arrived(part_in.at[: N_COL - 1], g_recv)
 
     def row_close(i, carry):
         acc = x[i].reshape(512, D).astype(F32)
@@ -240,35 +231,36 @@
         upd[i] = acc.reshape(N_ROW, CHUNKS, CHUNK, D)
         return carry
 
-    lax.fori_loop(0, ROW_DEV, row_close, 0)
-
-    back.append(column_pass(1))
+    with jax.named_scope('row_close'):
+        lax.fori_loop(0, ROW_DEV, row_close, 0, unroll=True)
+
+    with jax.named_scope('col_b'):
+        column_pass(1)
 
     for h in range(CHUNKS):
-        for copy in back[h]:
-            copy.wait_recv()
-
-        def transition(i, carry):
-            u = (upd[i, :, h] + ret[h, :, i].astype(F32)).reshape(256, D)
-            t = normalize(u, tg[...]).astype(BF16)
-            hid = dot(t, up[...])
-            hid = (hid * sigmoid(hid)).astype(BF16)
-            out_ref[i, :, h] = (u + dot(hid, down[...])).astype(BF16).reshape(N_ROW, CHUNK, D)
-            return carry
-
-        lax.fori_loop(0, ROW_DEV, transition, 0)
-
-    for copy in sends + scatter + gather + back[0] + back[1]:
-        copy.wait_send()
+        for half in range(2):
+            with jax.named_scope("r_wait"):
+                arrived(ret.at[h, : N_ROW - 1, pl.ds(2 * half, 2)], r_recv.at[h, half])
+            with jax.named_scope("trans"):
+                for i in (2 * half, 2 * half + 1):
+                    u = (upd[i, :, h] + ret[h, :, i].astype(F32)).reshape(256, D)
+                    t = normalize(u, tg[...]).astype(BF16)
+                    hid = dot(t, up[...])
+                    hid = (hid * sigmoid(hid)).astype(BF16)
+                    out_ref[i, :, h] = (u + dot(hid, down[...])).astype(BF16).reshape(N_ROW, CHUNK, D)
+
+    arrived(col_in.at[:, : N_ROW - 1], f_send)
+    arrived(part_in.at[: N_COL - 1], s_send)
+    arrived(part_in.at[: N_COL - 1], g_send)
+    arrived(col_out.at[:, : N_ROW - 1], r_send)
 
 
 def shards(x, norm_gain, in_weights, head_gain, out_weights, trans_gain, up_weight, down_weight):
-    any_spec = pl.BlockSpec(memory_space=pl.ANY)
-    n, m = len(ROW_STEPS), len(COL_STEPS)
+    any_spec = pl.BlockSpec(memory_space=pltpu.HBM)
     dma = pltpu.SemaphoreType.DMA
     out = pl.pallas_call(
         kernel,
-        out_shape=jax.ShapeDtypeStruct((ROW_DEV, N_ROW, CHUNKS, CHUNK, D), BF16),
+        out_shape=pltpu.VMEM((ROW_DEV, N_ROW, CHUNKS, CHUNK, D), BF16),
         in_specs=[any_spec] * 8,
         out_specs=pl.BlockSpec(memory_space=pltpu.VMEM),
         scratch_shapes=[
@@ -292,8 +284,8 @@
             pltpu.VMEM((64 * CHUNK, D), F32),
             pltpu.VMEM((CHUNKS, N_ROW, ROW_DEV, CHUNK, D), BF16),
             pltpu.VMEM((CHUNKS, N_ROW, ROW_DEV, CHUNK, D), BF16),
-            dma((8,)), dma((CHUNKS, n)), dma((CHUNKS, n)), dma((CHUNKS, n)), dma((CHUNKS, n)),
-            dma((CHUNKS,)), dma((m,)), dma((m,)), dma((m,)), dma((m,)),
+            dma((2,)), dma(()), dma((CHUNKS,)), dma(()), dma((CHUNKS, 2)),
+            dma(()), dma(()), dma(()), dma(()),
         ],
         compiler_params=pltpu.CompilerParams(
             collective_id=0, has_side_effects=True, vmem_limit_bytes=60 * 1024 * 1024

time: 41.6 us -> 37.2 us (0.89)
  Pallas kernels: 39.2 us -> 36 us
  local copies, waits for them, and re-layouts: 1.87 us -> 0.8 us
    pallas_call x1, Pallas kernels: 39.2 us -> 36 us  [shards(): pl.pallas_call(kernel, out_shape=pltpu.VMEM((ROW_DEV, N_ROW, CHUNKS, CHUN...]
    unnamed x1, local copies, waits for them, and re-layouts: 1.87 us -> 0.8 us
where the time goes in v2:
time: 37.2 us; the launch traced here: 36.8 us
  Pallas kernels  36 us (97%)
  local copies, waits for them, and re-layouts  0.8 us (2%)
    pallas_call x1, Pallas kernels, shards(): pl.pallas_call(kernel, out_shape=pltpu.VMEM((ROW_DEV, N_ROW, CHUNKS, CHUN...  36 us
    unnamed x1, local copies, waits for them, and re-layouts  0.8 us

profile of v2, /device:TPU:32, one launch (start us, length us, event | category | flops | bytes accessed | tf_op | source)
XLA Modules:
  0.0 36.8 jit_solution(7061833562961540198)
XLA Ops:
  0.0 36.0 %shard_map.82 = bf16[4,16,2,16,128]{4,3,2,1,0:T(8,128)(2,1)S(1)} custom-call(bf16[4,16,2,16,128]{4,3,2,1,0:T(8,128)(2,1)} %bitcast.5, f32[1,128]{1,0:T(1,128)} %bitcast.6, bf16[3,128,512]{2,1,0:T(8,128)(2,1)} %win_hbm.1, f32[3,128]{1,0:T(4,128)} %hg_hbm.1, bf16[3,128,128]{2,1,0:T(8,128)(2,1)} %wout_hbm.1, f32[1,128]{1,0:T(1,128)} %bitcast.7, ...), custom_call_target="tpu_custom_call" | custom-call | tf_op jit(solution)/shard_map/pallas_call | solution.py:261
  36.0 0.8 %copy.10 = bf16[4,512,128]{2,1,0:T(8,128)(2,1)} copy(bf16[4,512,128]{2,1,0:T(8,128)(2,1)S(1)} %bitcast.4) | data formatting | bytes 1048576

commit v3 on v2

v3 whole, which is shorter than its diff:
```python
import jax
import jax.numpy as jnp
from jax import lax
from jax.experimental import pallas as pl
from jax.experimental.pallas import tpu as pltpu
from jax.sharding import PartitionSpec as P

D = 128
HEADS = 4
HEAD = 32
FF = 512
N_ROW = 16
N_COL = 16
ROW_DEV = 4
UNITS = 4
UNIT = 8
FORWARD = [(0, 1), (1, 2), (2, 3), (3, 4)]
BACK = [[((0, 1), (0, 4)), ((1, 2), (0, 4))], [((2, 3), (0, 4)), ((3, 4), (0, 2)), ((3, 4), (2, 4))]]
EPS = 1e-05
MESH = pl.DeviceIdType.MESH
F32 = jnp.float32
BF16 = jnp.bfloat16

ROW_STAGES = [
    [(0, 2), (0, 6), (0, 1), (0, 7), (1, 0)],
    [(0, 4), (0, 3), (0, 5), (1, 2), (1, 6), (1, 1), (1, 7)],
    [(1, 4), (1, 3), (1, 5)],
]
ROW_STEPS = [step for stage in ROW_STAGES[::-1] for step in stage]
COL_STEPS = [
    (dx, dl, dc) for dx in (2, 1, 3, 0) for dl in (1, 0) for dc in (1, 0) if (dx, dl, dc) != (0, 0, 0)
]
FILL = ([(k, step) for k in (1, 2, 3) for step in ROW_STAGES[0][:4]], [])
COL_NEXT = [(1, 0, 0), (3, 0, 0), (0, 1, 0), (0, 0, 1)]


def arrived(ref, sem):
    pltpu.make_async_copy(ref, ref, sem).wait()


def dot(a, b):
    return jnp.dot(a, b, preferred_element_type=F32)


def dot_t(a, b):
    return lax.dot_general(a, b, (((1,), (1,)), ((), ())), preferred_element_type=F32)


def feature(v):
    return jnp.maximum(v, 0.0) + jnp.exp(jnp.minimum(v, 0.0))


def sigmoid(v):
    return 0.5 * jnp.tanh(0.5 * v) + 0.5


def normalize(v, gain):
    meansq = jnp.mean(v * v, axis=-1, keepdims=True)
    return v * lax.rsqrt(meansq + EPS) * gain


def same_head(rows, columns):
    r = lax.broadcasted_iota(jnp.int32, (rows, columns), 0) % D // HEAD
    c = lax.broadcasted_iota(jnp.int32, (rows, columns), 1) % D // HEAD
    return r == c


def kernel(
    x_hbm, ng_hbm, win_hbm, hg_hbm, wout_hbm, tg_hbm, up_hbm, down_hbm,
    out_ref,
    x, ng, win, hg, wout, tg, up, down,
    wkt, q_keep, gate_keep, upd,
    part, part_in, state, col_in, col_norm, col_res, col_out, ret,
    local_sem, f_send, f_recv, r_send, r_recv, s_send, s_recv, g_send, g_recv, row_in, col_told,
):
    row = lax.axis_index("row")
    col = lax.axis_index("col")
    y_hi, z = row // 8, row % 8
    cx, cl, cc = col // 4, (col // 2) % 2, col % 2

    def row_peer(step):
        return ((y_hi + step[0]) % 2) * 8 + (z + step[1]) % 8

    def col_peer(step):
        return ((cx + step[0]) % 4) * 4 + ((cl + step[1]) % 2) * 2 + (cc + step[2]) % 2

    loads = [
        pltpu.make_async_copy(src, dst, local_sem.at[int(k > 0)])
        for k, (src, dst) in enumerate(
            [
                (x_hbm, x), (ng_hbm, ng), (win_hbm, win), (hg_hbm, hg),
                (wout_hbm, wout), (tg_hbm, tg), (up_hbm, up), (down_hbm, down),
            ]
        )
    ]
    for load in loads:
        load.start()
    for k, (u0, u1) in enumerate(FORWARD):
        units = pl.ds(u0, u1 - u0)
        pltpu.make_async_copy(
            x_hbm.at[:, row, units], col_in.at[row, :, units], f_recv.at[k]
        ).start()

    def send_forward(k, step):
        peer = row_peer(step)
        units = pl.ds(FORWARD[k][0], FORWARD[k][1] - FORWARD[k][0])
        pltpu.make_async_remote_copy(
            src_ref=x_hbm.at[:, peer, units],
            dst_ref=col_in.at[row, :, units],
            send_sem=f_send,
            recv_sem=f_recv.at[k],
            device_id=(peer, col),
            device_id_type=MESH,
        ).start()

    def tell_row(sem, steps):
        for step in steps:
            pl.semaphore_signal(sem, 1, device_id=(row_peer(step), col), device_id_type=MESH)

    def tell_col(sem):
        for step in COL_NEXT:
            pl.semaphore_signal(sem, 1, device_id=(row, col_peer(step)), device_id_type=MESH)

    barrier = pltpu.get_barrier_semaphore()
    tell_row(barrier, ROW_STAGES[0])
    tell_col(barrier)
    with jax.named_scope("bar"):
        pl.semaphore_wait(barrier, len(ROW_STAGES[0]) + len(COL_NEXT))
    near = ROW_STAGES[0][:4]
    tell_row(row_in.at[0], near)
    tell_col(col_told.at[0])
    for step in ROW_STAGES[0]:
        send_forward(0, step)
    for k, step in FILL[0]:
        send_forward(k, step)
    with jax.named_scope("stage"):
        pl.semaphore_wait(row_in.at[0], len(near))
    tell_row(row_in.at[1], [(1, 0)])
    for step in ROW_STAGES[1]:
        send_forward(0, step)
    for k, step in FILL[1]:
        send_forward(k, step)
    pl.semaphore_wait(col_told.at[0], len(COL_NEXT))
    tell_col(col_told.at[1])
    with jax.named_scope("stage"):
        pl.semaphore_wait(row_in.at[1], 1)
    for step in ROW_STAGES[2]:
        send_forward(0, step)
    for k in range(1, len(FORWARD)):
        for step in ROW_STEPS:
            if (k, step) not in FILL[0] + FILL[1]:
                send_forward(k, step)
    pl.semaphore_wait(col_told.at[1], len(COL_NEXT))
    tell_col(col_told.at[2])

    with jax.named_scope("loads"):
      for load in loads:
        load.wait()
    for p in range(3):
        wkt[p] = win[p, :, D : 2 * D].astype(F32).T.astype(BF16)

    head_mask = same_head(D, D)

    def row_open(i, carry):
        normed = normalize(x[i].reshape(512, D).astype(F32), ng[...]).astype(BF16)
        for p in range(2):
            q_keep[p, i] = feature(dot(normed, win[p, :, :D])).astype(BF16)
            key_t = feature(dot_t(wkt[p], normed)).astype(BF16)
            tail = dot(normed, win[p, :, 2 * D :])
            gate_keep[p, i] = sigmoid(tail[:, D:])
            full = dot(key_t, tail[:, :D].astype(BF16))
            full = jnp.where(head_mask, full, 0.0).reshape(HEADS, HEAD, D).sum(axis=0)
            part[p, i] = full.astype(BF16)
        return carry

    with jax.named_scope('row_open'):
        lax.fori_loop(0, ROW_DEV, row_open, 0, unroll=True)
    pl.semaphore_wait(col_told.at[2], len(COL_NEXT))

    def slice_of(ref, at):
        return ref.at[at // 8, (at // 2) % 4, pl.ds((at % 2) * 16, 16)]

    for step in COL_STEPS:
        peer = col_peer(step)
        pltpu.make_async_remote_copy(
            src_ref=slice_of(part, peer),
            dst_ref=part_in.at[col],
            send_sem=s_send,
            recv_sem=s_recv,
            device_id=(row, peer),
            device_id_type=MESH,
        ).start()
    part_in[col] = slice_of(part, col)[...]

    first_half = lax.broadcasted_iota(jnp.int32, (D, D), 0) < 64
    pair_mask = same_head(D, 2 * D)

    def column_pass(u):
        block = col_in[:, :, u].reshape(64 * UNIT, D).astype(F32)
        col_norm[...] = normalize(block, ng[...])
        for group in range(UNIT // 4):
            normed = jnp.concatenate(
                [col_norm[pl.ds(4 * group + c, 64, stride=UNIT), :] for c in range(4)], axis=0
            ).astype(BF16)
            query = feature(dot(normed, win[2, :, :D])).astype(BF16)
            key_t = feature(dot_t(wkt[2], normed)).astype(BF16)
            tail = dot(normed, win[2, :, 2 * D :])
            value = tail[:, :D].astype(BF16)
            heads = []
            for pair in range(2):
                at = slice(D * pair, D * pair + D)
                v = value[at]
                zero = jnp.zeros_like(v)
                v2 = jnp.concatenate(
                    [jnp.where(first_half, v, zero), jnp.where(first_half, zero, v)], axis=1
                )
                s = jnp.where(pair_mask, dot(key_t[:, at], v2), 0.0).astype(BF16)
                o = dot(query[at], s)
                heads += [o[:64, :D], o[64:, D:]]
            mixed = normalize(jnp.concatenate(heads, axis=0), hg[2:3]) * sigmoid(tail[:, D:])
            res = dot(mixed.astype(BF16), wout[2])
            for c in range(4):
                col_res[pl.ds(4 * group + c, 64, stride=UNIT), :] = res[64 * c : 64 * c + 64]
        col_out[:, :, u] = col_res[...].astype(BF16).reshape(N_ROW, ROW_DEV, UNIT, D)

    groups = [group for groups in BACK for group in groups]

    def send_back(g):
        (u0, u1), (i0, i1) = groups[g]
        rows, units = pl.ds(i0, i1 - i0), pl.ds(u0, u1 - u0)
        for step in ROW_STEPS:
            peer = row_peer(step)
            pltpu.make_async_remote_copy(
                src_ref=col_out.at[peer, rows, units],
                dst_ref=ret.at[row, rows, units],
                send_sem=r_send,
                recv_sem=r_recv.at[g],
                device_id=(peer, col),
                device_id_type=MESH,
            ).start()

    def column_chunk(k):
        with jax.named_scope("f_wait"):
            arrived(col_in.at[:, :, pl.ds(FORWARD[k][0], FORWARD[k][1] - FORWARD[k][0])], f_recv.at[k])
        for u in range(*FORWARD[k]):
            with jax.named_scope("col_pass"):
                column_pass(u)
            for g, ((u0, u1), _) in enumerate(groups):
                if u1 == u + 1:
                    send_back(g)
            ret[row, :, u] = col_out[row, :, u]

    column_chunk(0)

    with jax.named_scope("rs_wait"):
        arrived(part_in.at[: N_COL - 1], s_recv)
    total = part_in[...].astype(F32).sum(axis=0)
    slice_of(state, col)[...] = total.astype(BF16)
    for step in COL_STEPS:
        peer = col_peer(step)
        pltpu.make_async_remote_copy(
            src_ref=slice_of(state, col),
            dst_ref=slice_of(state, col),
            send_sem=g_send,
            recv_sem=g_recv,
            device_id=(row, peer),
            device_id_type=MESH,
        ).start()

    for k in range(1, len(FORWARD)):
        column_chunk(k)

    with jax.named_scope("ag_wait"):
        arrived(part_in.at[: N_COL - 1], g_recv)

    def row_close(i, carry):
        acc = x[i].reshape(512, D).astype(F32)
        for p in range(2):
            s = state[p, i]
            s = jnp.concatenate([s, s, s, s], axis=0)
            s = jnp.where(head_mask, s, jnp.zeros_like(s))
            mixed = normalize(dot(q_keep[p, i], s), hg[p : p + 1]) * gate_keep[p, i]
            acc = acc + dot(mixed.astype(BF16), wout[p]).astype(BF16).astype(F32)
        upd[i] = acc.reshape(N_ROW, UNITS, UNIT, D)
        return carry

    with jax.named_scope('row_close'):
        lax.fori_loop(0, ROW_DEV, row_close, 0, unroll=True)

    for g, ((u0, u1), (i0, i1)) in enumerate(groups):
        with jax.named_scope("r_wait"):
            arrived(ret.at[: N_ROW - 1, pl.ds(i0, i1 - i0), pl.ds(u0, u1 - u0)], r_recv.at[g])
        with jax.named_scope("trans"):
            for u in range(u0, u1):
                for i in range(i0, i1, 2):
                    both = [upd[r, :, u] + ret[:, r, u].astype(F32) for r in (i, i + 1)]
                    v = jnp.concatenate(both, axis=0).reshape(2 * N_ROW * UNIT, D)
                    t = normalize(v, tg[...]).astype(BF16)
                    hid = dot(t, up[...])
                    hid = (hid * sigmoid(hid)).astype(BF16)
                    res = (v + dot(hid, down[...])).astype(BF16).reshape(2, N_ROW, UNIT, D)
                    out_ref[i, :, u] = res[0]
                    out_ref[i + 1, :, u] = res[1]

    arrived(col_in.at[: N_ROW - 1], f_send)
    arrived(part_in.at[: N_COL - 1], s_send)
    arrived(part_in.at[: N_COL - 1], g_send)
    arrived(col_out.at[: N_ROW - 1], r_send)


def shards(x, norm_gain, in_weights, head_gain, out_weights, trans_gain, up_weight, down_weight):
    any_spec = pl.BlockSpec(memory_space=pltpu.HBM)
    dma = pltpu.SemaphoreType.DMA
    out = pl.pallas_call(
        kernel,
        out_shape=pltpu.VMEM((ROW_DEV, N_ROW, UNITS, UNIT, D), BF16),
        in_specs=[any_spec] * 8,
        out_specs=pl.BlockSpec(memory_space=pltpu.VMEM),
        scratch_shapes=[
            pltpu.VMEM((ROW_DEV, N_ROW, UNITS, UNIT, D), BF16),
            pltpu.VMEM((1, D), F32),
            pltpu.VMEM((3, D, 4 * D), BF16),
            pltpu.VMEM((3, D), F32),
            pltpu.VMEM((3, D, D), BF16),
            pltpu.VMEM((1, D), F32),
            pltpu.VMEM((D, FF), BF16),
            pltpu.VMEM((FF, D), BF16),
            pltpu.VMEM((3, D, D), BF16),
            pltpu.VMEM((2, ROW_DEV, 512, D), BF16),
            pltpu.VMEM((2, ROW_DEV, 512, D), F32),
            pltpu.VMEM((ROW_DEV, N_ROW, UNITS, UNIT, D), F32),
            pltpu.VMEM((2, ROW_DEV, HEAD, D), BF16),
            pltpu.VMEM((N_COL, 16, D), BF16),
            pltpu.VMEM((2, ROW_DEV, HEAD, D), BF16),
            pltpu.VMEM((N_ROW, ROW_DEV, UNITS, UNIT, D), BF16),
            pltpu.VMEM((64 * UNIT, D), F32),
            pltpu.VMEM((64 * UNIT, D), F32),
            pltpu.VMEM((N_ROW, ROW_DEV, UNITS, UNIT, D), BF16),
            pltpu.VMEM((N_ROW, ROW_DEV, UNITS, UNIT, D), BF16),
            dma((2,)), dma(()), dma((len(FORWARD),)), dma(()), dma((sum(map(len, BACK)),)),
            dma(()), dma(()), dma(()), dma(()),
            pltpu.SemaphoreType.REGULAR((2,)), pltpu.SemaphoreType.REGULAR((3,)),
        ],
        compiler_params=pltpu.CompilerParams(
            collective_id=0, has_side_effects=True, vmem_limit_bytes=60 * 1024 * 1024
        ),
    )(
        x.reshape(ROW_DEV, N_ROW, UNITS, UNIT, D), norm_gain.reshape(1, D), in_weights, head_gain,
        out_weights, trans_gain.reshape(1, D), up_weight, down_weight,
    )
    return out.reshape(x.shape)


def solution(mesh):
    in_specs = (P("row", "col", None), P(), P(), P(), P(), P(), P(), P())
    return jax.shard_map(
        shards, mesh=mesh, in_specs=in_specs, out_specs=P("row", "col", None), check_vma=False
    )
```

time: 37.2 us -> 35.7 us (0.960)
  Pallas kernels: 36 us -> 34.8 us
    pallas_call x1, Pallas kernels: 36 us -> 34.8 us  [shards(): pl.pallas_call(kernel, out_shape=pltpu.VMEM((ROW_DEV, N_ROW, UNITS, UNIT,...]
where the time goes in v3:
time: 35.7 us; the launch traced here: 35.6 us
  Pallas kernels  34.8 us (97%)
  local copies, waits for them, and re-layouts  0.8 us (2%)
    pallas_call x1, Pallas kernels, shards(): pl.pallas_call(kernel, out_shape=pltpu.VMEM((ROW_DEV, N_ROW, UNITS, UNIT,...  34.8 us
    unnamed x1, local copies, waits for them, and re-layouts  0.8 us

profile of v3, /device:TPU:32, one launch (start us, length us, event | category | flops | bytes accessed | tf_op | source)
XLA Modules:
  0.0 35.6 jit_solution(17673343630364564511)
XLA Ops:
  0.0 34.8 %shard_map.82 = bf16[4,16,4,8,128]{4,3,2,1,0:T(8,128)(2,1)S(1)} custom-call(bf16[4,16,4,8,128]{4,3,2,1,0:T(8,128)(2,1)} %bitcast.5, f32[1,128]{1,0:T(1,128)} %bitcast.6, bf16[3,128,512]{2,1,0:T(8,128)(2,1)} %win_hbm.1, f32[3,128]{1,0:T(4,128)} %hg_hbm.1, bf16[3,128,128]{2,1,0:T(8,128)(2,1)} %wout_hbm.1, f32[1,128]{1,0:T(1,128)} %bitcast.7, ...), custom_call_target="tpu_custom_call" | custom-call | tf_op jit(solution)/shard_map/pallas_call | solution.py:314
  34.8 0.8 %copy.10 = bf16[4,512,128]{2,1,0:T(8,128)(2,1)} copy(bf16[4,512,128]{2,1,0:T(8,128)(2,1)S(1)} %bitcast.4) | data formatting | bytes 1048576

commit v4 on v3

--- a/solution.py
+++ b/solution.py
@@ -27,6 +27,8 @@
     [(1, 4), (1, 3), (1, 5)],
 ]
 ROW_STEPS = [step for stage in ROW_STAGES[::-1] for step in stage]
+FAR, NEAR = ROW_STEPS[:8], ROW_STEPS[8:]
+ISSUE = [[(0, ROW_STEPS)], [(1, ROW_STEPS)], [(2, FAR)], [(3, FAR), (4, FAR), (2, NEAR), (3, NEAR), (4, NEAR)]]
 COL_STEPS = [
     (dx, dl, dc) for dx in (2, 1, 3, 0) for dl in (1, 0) for dc in (1, 0) if (dx, dl, dc) != (0, 0, 0)
 ]
@@ -59,6 +61,12 @@
     return v * lax.rsqrt(meansq + EPS) * gain
 
 
+def transition(v, tg, up, down):
+    hid = dot(normalize(v, tg[...]).astype(BF16), up[...])
+    hid = (hid * sigmoid(hid)).astype(BF16)
+    return (v + dot(hid, down[...])).astype(BF16)
+
+
 def same_head(rows, columns):
     r = lax.broadcasted_iota(jnp.int32, (rows, columns), 0) % D // HEAD
     c = lax.broadcasted_iota(jnp.int32, (rows, columns), 1) % D // HEAD
@@ -67,8 +75,8 @@
 
 def kernel(
     x_hbm, ng_hbm, win_hbm, hg_hbm, wout_hbm, tg_hbm, up_hbm, down_hbm,
-    out_ref,
-    x, ng, win, hg, wout, tg, up, down,
+    out_ref, last, tg, up, down,
+    x, ng, win, hg, wout,
     wkt, q_keep, gate_keep, upd,
     part, part_in, state, col_in, col_norm, col_res, col_out, ret,
     local_sem, f_send, f_recv, r_send, r_recv, s_send, s_recv, g_send, g_recv, row_in, col_told,
@@ -225,10 +233,10 @@
 
     groups = [group for groups in BACK for group in groups]
 
-    def send_back(g):
+    def send_back(g, steps):
         (u0, u1), (i0, i1) = groups[g]
         rows, units = pl.ds(i0, i1 - i0), pl.ds(u0, u1 - u0)
-        for step in ROW_STEPS:
+        for step in steps:
             peer = row_peer(step)
             pltpu.make_async_remote_copy(
                 src_ref=col_out.at[peer, rows, units],
@@ -245,9 +253,8 @@
         for u in range(*FORWARD[k]):
             with jax.named_scope("col_pass"):
                 column_pass(u)
-            for g, ((u0, u1), _) in enumerate(groups):
-                if u1 == u + 1:
-                    send_back(g)
+            for g, steps in ISSUE[u]:
+                send_back(g, steps)
             ret[row, :, u] = col_out[row, :, u]
 
     column_chunk(0)
@@ -295,12 +302,12 @@
                 for i in range(i0, i1, 2):
                     both = [upd[r, :, u] + ret[:, r, u].astype(F32) for r in (i, i + 1)]
                     v = jnp.concatenate(both, axis=0).reshape(2 * N_ROW * UNIT, D)
-                    t = normalize(v, tg[...]).astype(BF16)
-                    hid = dot(t, up[...])
-                    hid = (hid * sigmoid(hid)).astype(BF16)
-                    res = (v + dot(hid, down[...])).astype(BF16).reshape(2, N_ROW, UNIT, D)
-                    out_ref[i, :, u] = res[0]
-                    out_ref[i + 1, :, u] = res[1]
+                    if g == len(groups) - 1:
+                        last[...] = v
+                    else:
+                        res = transition(v, tg, up, down).reshape(2, N_ROW, UNIT, D)
+                        out_ref[i, :, u] = res[0]
+                        out_ref[i + 1, :, u] = res[1]
 
     arrived(col_in.at[: N_ROW - 1], f_send)
     arrived(part_in.at[: N_COL - 1], s_send)
@@ -308,23 +315,40 @@
     arrived(col_out.at[: N_ROW - 1], r_send)
 
 
+def finish(most, last, tg, up, down, out, rest, sem):
+    copies = [
+        pltpu.make_async_copy(most.at[i, :, :3], out.at[i, :, :3], sem.at[i]) for i in range(ROW_DEV)
+    ]
+    copies.append(pltpu.make_async_copy(most.at[:2, :, 3], out.at[:2, :, 3], sem.at[4]))
+    for copy in copies:
+        copy.start()
+    rest[...] = transition(last[...], tg, up, down).reshape(2, N_ROW, UNIT, D)
+    copies.append(pltpu.make_async_copy(rest, out.at[2:, :, 3], sem.at[5]))
+    copies[-1].start()
+    for copy in copies:
+        copy.wait()
+
+
 def shards(x, norm_gain, in_weights, head_gain, out_weights, trans_gain, up_weight, down_weight):
-    any_spec = pl.BlockSpec(memory_space=pltpu.HBM)
+    any_spec = pl.BlockSpec(memory_space=pl.ANY)
     dma = pltpu.SemaphoreType.DMA
-    out = pl.pallas_call(
+    parts = pl.pallas_call(
         kernel,
-        out_shape=pltpu.VMEM((ROW_DEV, N_ROW, UNITS, UNIT, D), BF16),
+        out_shape=[
+            pltpu.VMEM((ROW_DEV, N_ROW, UNITS, UNIT, D), BF16),
+            pltpu.VMEM((2 * N_ROW * UNIT, D), F32),
+            pltpu.VMEM((1, D), F32),
+            pltpu.VMEM((D, FF), BF16),
+            pltpu.VMEM((FF, D), BF16),
+        ],
         in_specs=[any_spec] * 8,
-        out_specs=pl.BlockSpec(memory_space=pltpu.VMEM),
+        out_specs=[pl.BlockSpec(memory_space=pltpu.VMEM)] * 5,
         scratch_shapes=[
             pltpu.VMEM((ROW_DEV, N_ROW, UNITS, UNIT, D), BF16),
             pltpu.VMEM((1, D), F32),
             pltpu.VMEM((3, D, 4 * D), BF16),
             pltpu.VMEM((3, D), F32),
             pltpu.VMEM((3, D, D), BF16),
-            pltpu.VMEM((1, D), F32),
-            pltpu.VMEM((D, FF), BF16),
-            pltpu.VMEM((FF, D), BF16),
             pltpu.VMEM((3, D, D), BF16),
             pltpu.VMEM((2, ROW_DEV, 512, D), BF16),
             pltpu.VMEM((2, ROW_DEV, 512, D), F32),
@@ -348,6 +372,14 @@
         x.reshape(ROW_DEV, N_ROW, UNITS, UNIT, D), norm_gain.reshape(1, D), in_weights, head_gain,
         out_weights, trans_gain.reshape(1, D), up_weight, down_weight,
     )
+    out = pl.pallas_call(
+        finish,
+        out_shape=jax.ShapeDtypeStruct((ROW_DEV, N_ROW, UNITS, UNIT, D), BF16),
+        in_specs=[pl.BlockSpec(memory_space=pltpu.VMEM)] * 5,
+        out_specs=any_spec,
+        scratch_shapes=[pltpu.VMEM((2, N_ROW, UNIT, D), BF16), dma((6,))],
+        compiler_params=pltpu.CompilerParams(vmem_limit_bytes=8 * 1024 * 1024),
+    )(*(pltpu.with_memory_space_constraint(part, pltpu.VMEM) for part in parts))
     return out.reshape(x.shape)
 
 

time: 35.7 us -> 35.5 us (level); the launches traced: 35.6 us -> 35 us
  local copies, waits for them, and re-layouts: 0.8 us -> 0 us
    unnamed x1 -> x0, local copies, waits for them, and re-layouts: 0.8 us -> none
    pallas_call x1 -> x2, Pallas kernels: 34.8 us -> 35 us  [the longest x1 33.9 us: shards(): pl.pallas_call(kernel, out_shape=[pltpu.VMEM((ROW_DEV, N_ROW, UNITS, UNIT...]
where the time goes in v4:
time: 35.5 us; the launch traced here: 35 us
  Pallas kernels  35 us (99%)
    pallas_call x1, Pallas kernels, shards(): pl.pallas_call(kernel, out_shape=[pltpu.VMEM((ROW_DEV, N_ROW, UNITS, UNIT...  33.9 us
    pallas_call x1, Pallas kernels, shards(): pl.pallas_call(finish, out_shape=jax.ShapeDtypeStruct((ROW_DEV, N_ROW, UN...  1.15 us

profile of v4, /device:TPU:32, one launch (start us, length us, event | category | flops | bytes accessed | tf_op | source)
XLA Modules:
  0.0 35.0 jit_solution(6702030442143739921)
XLA Ops:
  0.0 33.9 %shard_map.82 = (bf16[4,16,4,8,128]{4,3,2,1,0:T(8,128)(2,1)S(1)}, f32[256,128]{1,0:T(8,128)S(1)}, f32[1,128]{1,0:T(1,128)S(1)}, bf16[128,512]{1,0:T(8,128)(2,1)S(1)}, bf16[512,128]{1,0:T(8,128)(2,1)S(1)}) custom-call(bf16[4,16,4,8,128]{4,3,2,1,0:T(8,128)(2,1)} %bitcast.4, f32[1,128]{1,0:T(1,128)} %bitcast.5, bf16[3,128,512]{2,1,0:T(8,128)(2,1)} %win_hbm.1, ...), custom_call_target="tpu_custom_call" | custom-call | tf_op jit(solution)/shard_map/pallas_call | solution.py:335
  33.9 1.2 %shard_map.83 = bf16[4,16,4,8,128]{4,3,2,1,0:T(8,128)(2,1)} custom-call(bf16[4,16,4,8,128]{4,3,2,1,0:T(8,128)(2,1)S(1)} %get-tuple-element.10.most, f32[256,128]{1,0:T(8,128)S(1)} %get-tuple-element.11.last, f32[1,128]{1,0:T(1,128)S(1)} %get-tuple-element.12.tg, bf16[128,512]{1,0:T(8,128)(2,1)S(1)} %get-tuple-element.13.up, ...), custom_call_target="tpu_custom_call" | custom-call | tf_op jit(solution)/shard_map/pallas_call | solution.py:375

commit v5 on v4

--- a/solution.py
+++ b/solution.py
@@ -14,7 +14,7 @@
 ROW_DEV = 4
 UNITS = 4
 UNIT = 8
-FORWARD = [(0, 1), (1, 2), (2, 3), (3, 4)]
+FORWARD = [(0, 1), (1, 2), (2, 4)]
 BACK = [[((0, 1), (0, 4)), ((1, 2), (0, 4))], [((2, 3), (0, 4)), ((3, 4), (0, 2)), ((3, 4), (2, 4))]]
 EPS = 1e-05
 MESH = pl.DeviceIdType.MESH
@@ -32,7 +32,7 @@
 COL_STEPS = [
     (dx, dl, dc) for dx in (2, 1, 3, 0) for dl in (1, 0) for dc in (1, 0) if (dx, dl, dc) != (0, 0, 0)
 ]
-FILL = ([(k, step) for k in (1, 2, 3) for step in ROW_STAGES[0][:4]], [])
+FILL = ([(k, step) for k in (1, 2) for step in ROW_STAGES[0][:4]], [])
 COL_NEXT = [(1, 0, 0), (3, 0, 0), (0, 1, 0), (0, 0, 1)]
 
 
@@ -92,6 +92,17 @@
     def col_peer(step):
         return ((cx + step[0]) % 4) * 4 + ((cl + step[1]) % 2) * 2 + (cc + step[2]) % 2
 
+    def tell_row(sem, steps):
+        for step in steps:
+            pl.semaphore_signal(sem, 1, device_id=(row_peer(step), col), device_id_type=MESH)
+
+    def tell_col(sem):
+        for step in COL_NEXT:
+            pl.semaphore_signal(sem, 1, device_id=(row, col_peer(step)), device_id_type=MESH)
+
+    barrier = pltpu.get_barrier_semaphore()
+    tell_row(barrier, ROW_STAGES[0])
+    tell_col(barrier)
     loads = [
         pltpu.make_async_copy(src, dst, local_sem.at[int(k > 0)])
         for k, (src, dst) in enumerate(
@@ -121,17 +132,6 @@
             device_id_type=MESH,
         ).start()
 
-    def tell_row(sem, steps):
-        for step in steps:
-            pl.semaphore_signal(sem, 1, device_id=(row_peer(step), col), device_id_type=MESH)
-
-    def tell_col(sem):
-        for step in COL_NEXT:
-            pl.semaphore_signal(sem, 1, device_id=(row, col_peer(step)), device_id_type=MESH)
-
-    barrier = pltpu.get_barrier_semaphore()
-    tell_row(barrier, ROW_STAGES[0])
-    tell_col(barrier)
     with jax.named_scope("bar"):
         pl.semaphore_wait(barrier, len(ROW_STAGES[0]) + len(COL_NEXT))
     near = ROW_STAGES[0][:4]
@@ -253,9 +253,9 @@
         for u in range(*FORWARD[k]):
             with jax.named_scope("col_pass"):
                 column_pass(u)
+            ret[row, :, u] = col_out[row, :, u]
             for g, steps in ISSUE[u]:
                 send_back(g, steps)
-            ret[row, :, u] = col_out[row, :, u]
 
     column_chunk(0)
 

time: 35.5 us -> 35 us (0.986); the launches traced: 35 us -> 34.9 us
  no operation moved by 1% of the time
where the time goes in v5:
time: 35 us; the launch traced here: 34.9 us
  Pallas kernels  34.9 us (100%)
    pallas_call x1, Pallas kernels, shards(): pl.pallas_call(kernel, out_shape=[pltpu.VMEM((ROW_DEV, N_ROW, UNITS, UNIT...  33.7 us
    pallas_call x1, Pallas kernels, shards(): pl.pallas_call(finish, out_shape=jax.ShapeDtypeStruct((ROW_DEV, N_ROW, UN...  1.16 us

profile of v5, /device:TPU:32, one launch (start us, length us, event | category | flops | bytes accessed | tf_op | source)
XLA Modules:
  0.0 34.9 jit_solution(951510869850026146)
XLA Ops:
  0.0 33.7 %shard_map.82 = (bf16[4,16,4,8,128]{4,3,2,1,0:T(8,128)(2,1)S(1)}, f32[256,128]{1,0:T(8,128)S(1)}, f32[1,128]{1,0:T(1,128)S(1)}, bf16[128,512]{1,0:T(8,128)(2,1)S(1)}, bf16[512,128]{1,0:T(8,128)(2,1)S(1)}) custom-call(bf16[4,16,4,8,128]{4,3,2,1,0:T(8,128)(2,1)} %bitcast.4, f32[1,128]{1,0:T(1,128)} %bitcast.5, bf16[3,128,512]{2,1,0:T(8,128)(2,1)} %win_hbm.1, ...), custom_call_target="tpu_custom_call" | custom-call | tf_op jit(solution)/shard_map/pallas_call | solution.py:335
  33.7 1.2 %shard_map.83 = bf16[4,16,4,8,128]{4,3,2,1,0:T(8,128)(2,1)} custom-call(bf16[4,16,4,8,128]{4,3,2,1,0:T(8,128)(2,1)S(1)} %get-tuple-element.10.most, f32[256,128]{1,0:T(8,128)S(1)} %get-tuple-element.11.last, f32[1,128]{1,0:T(1,128)S(1)} %get-tuple-element.12.tg, bf16[128,512]{1,0:T(8,128)(2,1)S(1)} %get-tuple-element.13.up, ...), custom_call_target="tpu_custom_call" | custom-call | tf_op jit(solution)/shard_map/pallas_call | solution.py:375

commit v6 on v5

--- a/solution.py
+++ b/solution.py
@@ -302,8 +302,8 @@
                 for i in range(i0, i1, 2):
                     both = [upd[r, :, u] + ret[:, r, u].astype(F32) for r in (i, i + 1)]
                     v = jnp.concatenate(both, axis=0).reshape(2 * N_ROW * UNIT, D)
-                    if g == len(groups) - 1:
-                        last[...] = v
+                    if u == UNITS - 1:
+                        last[i * N_ROW * UNIT : (i + 2) * N_ROW * UNIT] = v
                     else:
                         res = transition(v, tg, up, down).reshape(2, N_ROW, UNIT, D)
                         out_ref[i, :, u] = res[0]
@@ -319,11 +319,10 @@
     copies = [
         pltpu.make_async_copy(most.at[i, :, :3], out.at[i, :, :3], sem.at[i]) for i in range(ROW_DEV)
     ]
-    copies.append(pltpu.make_async_copy(most.at[:2, :, 3], out.at[:2, :, 3], sem.at[4]))
     for copy in copies:
         copy.start()
-    rest[...] = transition(last[...], tg, up, down).reshape(2, N_ROW, UNIT, D)
-    copies.append(pltpu.make_async_copy(rest, out.at[2:, :, 3], sem.at[5]))
+    rest[...] = transition(last[...], tg, up, down).reshape(ROW_DEV, N_ROW, UNIT, D)
+    copies.append(pltpu.make_async_copy(rest, out.at[:, :, 3], sem.at[4]))
     copies[-1].start()
     for copy in copies:
         copy.wait()
@@ -336,7 +335,7 @@
         kernel,
         out_shape=[
             pltpu.VMEM((ROW_DEV, N_ROW, UNITS, UNIT, D), BF16),
-            pltpu.VMEM((2 * N_ROW * UNIT, D), F32),
+            pltpu.VMEM((ROW_DEV * N_ROW * UNIT, D), F32),
             pltpu.VMEM((1, D), F32),
             pltpu.VMEM((D, FF), BF16),
             pltpu.VMEM((FF, D), BF16),
@@ -377,7 +376,7 @@
         out_shape=jax.ShapeDtypeStruct((ROW_DEV, N_ROW, UNITS, UNIT, D), BF16),
         in_specs=[pl.BlockSpec(memory_space=pltpu.VMEM)] * 5,
         out_specs=any_spec,
-        scratch_shapes=[pltpu.VMEM((2, N_ROW, UNIT, D), BF16), dma((6,))],
+        scratch_shapes=[pltpu.VMEM((ROW_DEV, N_ROW, UNIT, D), BF16), dma((5,))],
         compiler_params=pltpu.CompilerParams(vmem_limit_bytes=8 * 1024 * 1024),
     )(*(pltpu.with_memory_space_constraint(part, pltpu.VMEM) for part in parts))
     return out.reshape(x.shape)

time: 35 us -> 35 us (level)
  no operation moved by 1% of the time
where the time goes in v6:
time: 35 us; the launch traced here: 34.9 us
  Pallas kernels  34.9 us (100%)
    pallas_call x1, Pallas kernels, shards(): pl.pallas_call(kernel, out_shape=[pltpu.VMEM((ROW_DEV, N_ROW, UNITS, UNIT...  33.6 us
    pallas_call x1, Pallas kernels, shards(): pl.pallas_call(finish, out_shape=jax.ShapeDtypeStruct((ROW_DEV, N_ROW, UN...  1.26 us

profile of v6, /device:TPU:32, one launch (start us, length us, event | category | flops | bytes accessed | tf_op | source)
XLA Modules:
  0.0 34.9 jit_solution(7642892448431449197)
XLA Ops:
  0.0 33.6 %shard_map.82 = (bf16[4,16,4,8,128]{4,3,2,1,0:T(8,128)(2,1)S(1)}, f32[512,128]{1,0:T(8,128)S(1)}, f32[1,128]{1,0:T(1,128)S(1)}, bf16[128,512]{1,0:T(8,128)(2,1)S(1)}, bf16[512,128]{1,0:T(8,128)(2,1)S(1)}) custom-call(bf16[4,16,4,8,128]{4,3,2,1,0:T(8,128)(2,1)} %bitcast.4, f32[1,128]{1,0:T(1,128)} %bitcast.5, bf16[3,128,512]{2,1,0:T(8,128)(2,1)} %win_hbm.1, ...), custom_call_target="tpu_custom_call" | custom-call | tf_op jit(solution)/shard_map/pallas_call | solution.py:334
  33.7 1.3 %shard_map.83 = bf16[4,16,4,8,128]{4,3,2,1,0:T(8,128)(2,1)} custom-call(bf16[4,16,4,8,128]{4,3,2,1,0:T(8,128)(2,1)S(1)} %get-tuple-element.10.most, f32[512,128]{1,0:T(8,128)S(1)} %get-tuple-element.11.last, f32[1,128]{1,0:T(1,128)S(1)} %get-tuple-element.12.tg, bf16[128,512]{1,0:T(8,128)(2,1)S(1)} %get-tuple-element.13.up, ...), custom_call_target="tpu_custom_call" | custom-call | tf_op jit(solution)/shard_map/pallas_call | solution.py:374
